TPU v7x, 32 devices: a whole 2x2x4 slice. The times are simulated.
32 devices in a mesh: groups: 2 (over x), exp: 16 (over z, y, core).
Axes of the slice: x: 2, y: 2, z: 4, core: 2. Of those that a mesh axis runs over, the one named last changes fastest.
Arguments:
- estimate: float32 [512, 4, 512], P('exp', 'groups'), parts along dimension 1, may hold values from -6 to 6
- observed: bfloat16 [32, 512, 512], P(('groups', 'exp')), parts along dimension 0, may hold values from -12 to 12
- pixel_mask: int32 [32, 512, 512], P(('groups', 'exp')), parts along dimension 0, may hold values 0 or 1
- blur_mix: float32 [32, 6, 8, 8], P(('groups', 'exp')), parts along dimension 0, may hold values from 0.2 to 1
- dithers: int32 [32, 2], P(('groups', 'exp')), parts along dimension 0, may hold values from -8 to 8, as said below
- patch_of: int32 [32], P(('groups', 'exp')), parts along dimension 0, may hold values from 0 to 1
- column_taps: bfloat16 [6, 15], replicated, may hold values from 0 to 0.119628906
- row_taps: bfloat16 [6, 15], replicated, may hold values from 0 to 0.119628906
Outputs:
- gradient: float32 [512, 4, 512], P('exp', 'groups'), parts along dimension 1
There are 2 independent parts, one for each index of `groups`. A program takes and returns all parts, laid end to end along the dimension named above; an argument that names none is the same for every part. Nothing has to cross between parts.
Inputs may be any that keep to these rules, and one draw needn't show every extreme that they name: `dithers`: each exposure's two offsets; the value 8 occurs among the row offsets and -8 among the column offsets.
All inputs are finite; a program needn't handle non-finite values. No bound on the sum of `pixel_mask` on one device may be relied on, other than what follows from the above.
Results may differ from a plain program's by a relative error of at most 0.004.
Values may be sent and summed in bfloat16 or wider, within the bound.
No kernel may reach another device: no remote copies, remote signals or barrier semaphores. Data moves between devices by JAX's collectives and lax.ppermute only.
A program may use at most 128 MiB of HBM per device.

v0:
```python
import jax
import jax.numpy as jnp
from jax import lax
from jax.sharding import PartitionSpec as P

DMAX = 8


def band_stack(tap_values, extent, col_offset):
    half_width = tap_values.shape[1] // 2
    source = lax.broadcasted_iota(jnp.int32, (extent, extent), 0)
    target = lax.broadcasted_iota(jnp.int32, (extent, extent), 1)
    offset = source - target - col_offset + half_width
    inside = (source - col_offset >= 0) & (source - col_offset < extent)
    running = jnp.zeros((tap_values.shape[0], extent, extent), jnp.float32)
    for tap_index in range(tap_values.shape[1]):
        matches = ((offset == tap_index) & inside).astype(jnp.float32)
        running = (
            running + tap_values[:, tap_index].astype(jnp.float32)[:, None, None] * matches[None]
        )
    return running.astype(jnp.bfloat16)


def exposure_back(rowed, frame_data, mask_frame, blur_weights, row_shift, column_band):
    extent = frame_data.shape[0]
    basis_count = blur_weights.shape[0]
    tile_count = blur_weights.shape[1]
    tile_side = extent // tile_count
    padded = jnp.pad(rowed, ((DMAX, DMAX), (0, 0)))
    shifted = lax.dynamic_slice_in_dim(padded, DMAX + row_shift, extent, 0).reshape(
        extent, basis_count, extent
    )
    blurred = jnp.einsum("kba,bkc->kac", column_band, shifted, preferred_element_type=jnp.float32)
    mix_full = jnp.broadcast_to(
        blur_weights[:, :, None, :, None],
        (basis_count, tile_count, tile_side, tile_count, tile_side),
    ).reshape(basis_count, extent, extent)
    model_image = jnp.sum(mix_full * blurred, axis=0)
    residual = mask_frame.astype(jnp.float32) * (model_image - frame_data.astype(jnp.float32))
    weighted = (mix_full * residual[None]).astype(jnp.bfloat16)
    backed = jnp.einsum("kab,kbc->akc", column_band, weighted, preferred_element_type=jnp.float32)
    backed = backed.astype(jnp.bfloat16).reshape(extent, basis_count * extent)
    return jnp.pad(backed, ((DMAX, DMAX), (0, 0)))


def back_rows(padded_back, back_stack, row_shift, patch_index, patch_count, first_row, row_count):
    picked = lax.dynamic_slice_in_dim(padded_back, first_row + DMAX - row_shift, row_count, 0)
    result = jnp.dot(picked, back_stack, preferred_element_type=jnp.float32)
    selector = lax.broadcasted_iota(jnp.int32, (1, patch_count, 1), 1) == patch_index
    return jnp.where(selector, result[:, None, :], jnp.zeros((), jnp.float32))


def per_device(estimate, observed, pixel_mask, blur_mix, dithers, patch_of, column_taps, row_taps):
    extent = observed.shape[1]
    patch_count = estimate.shape[1]
    band_rows = estimate.shape[0]
    row_shift = dithers[0, 0]
    column_shift = dithers[0, 1]
    patch_index = patch_of[0]
    column_band = band_stack(column_taps, extent, 0)
    row_band = band_stack(row_taps, extent, column_shift)
    forward_stack = jnp.transpose(row_band, (1, 0, 2)).reshape(extent, -1)
    back_stack = jnp.transpose(row_band, (0, 2, 1)).reshape(-1, extent)
    estimate_low = estimate.astype(jnp.bfloat16)
    gathered = lax.all_gather(estimate_low, "exp", axis=0, tiled=True)
    chosen = lax.dynamic_index_in_dim(gathered, patch_index, 1, keepdims=False)
    rowed = jnp.dot(chosen, forward_stack, preferred_element_type=jnp.float32).astype(jnp.bfloat16)
    padded_back = exposure_back(
        rowed, observed[0], pixel_mask[0], blur_mix[0], row_shift, column_band
    )
    complete = lax.psum(
        back_rows(padded_back, back_stack, row_shift, patch_index, patch_count, 0, extent), "exp"
    )
    return lax.dynamic_slice_in_dim(complete, lax.axis_index("exp") * band_rows, band_rows, 0)


def solution(mesh):
    in_specs = (
        P("exp", "groups", None),
        P(("groups", "exp"), None, None),
        P(("groups", "exp"), None, None),
        P(("groups", "exp"), None, None, None),
        P(("groups", "exp"), None),
        P(("groups", "exp")),
        P(),
        P(),
    )
    out_specs = P("exp", "groups", None)
    return jax.shard_map(
        per_device, mesh=mesh, in_specs=in_specs, out_specs=out_specs, check_vma=False
    )
```

profile of v0, /device:TPU:0, one launch (start us, length us, event | category | flops | bytes accessed | tf_op | source)
XLA Modules:
  0.0 287.0 jit_solution(5062200893745384783)
XLA Ops:
  10.3 7.4 %fusion.68 = (f32[512,512]{0,1:T(8,128)S(1)}, f32[512,512]{0,1:T(8,128)}, f32[512,512]{0,1:T(8,128)S(1)}, f32[512,512]{0,1:T(8,128)S(1)}, f32[512,512]{0,1:T(8,1...) fusion(s32[]{:T(128)} %bitcast.3, ...), kind=kLoop, calls=%fused_computation.95 | loop fusion | flops 25165824 | bytes 31457796 | tf_op jit(solution)/shard_map/convert_element_type | solution.py:17
  18.0 8.4 %add_convert_fusion = bf16[512,6,512]{0,2,1:T(8,128)(2,1)} fusion(f32[512,512]{0,1:T(8,128)S(1)} %get-tuple-element.51, f32[6]{0:T(128)S(1)} %get-tuple-element.33, f32[512,512]{0,1:T(8,128)S(1)} %get-tuple-element.52, f32[6]{0:T(128)S(1)} %get-tuple-element.34, f32[512,512]{0,1:T(8,128)S(1)} %get-tuple-element.53, f32[6]{0:T(128)S(1)} %get-tuple-element.21, ...), kind=kLoop, calls=%fused_computation.32 | loop fusion | flops 47185920 | bytes 18874728 | tf_op jit(solution)/shard_map/convert_element_type | solution.py:21
  26.4 7.0 %fusion.128 = (f32[512,512]{0,1:T(8,128)}, f32[512,512]{0,1:T(8,128)}, f32[512,512]{0,1:T(8,128)}, f32[512,512]{0,1:T(8,128)}, f32[512,512]{0,1:T(8,128)}, /*ind...) fusion(pred[512]{0:T(512)(128)(4,1)S(1)} %iota_compare_fusion), kind=kLoop, calls=%fused_computation.155 | loop fusion | flops 12320768 | bytes 15729152 | tf_op jit(solution)/shard_map/convert_element_type | solution.py:17
  38.8 2.6 copy.12
  41.4 2.5 copy.13
  44.0 2.6 copy.14
  46.5 2.5 copy.15
  51.6 2.6 copy.17
  54.1 2.5 copy.18
  56.7 2.6 copy.19
  61.8 2.5 copy.21
  64.3 2.6 copy.22
  66.9 2.6 copy.23
  69.5 2.5 copy.24
  72.0 2.5 copy.25
  74.5 5.4 %broadcast_in_dim.19 = f32[6,8,64,8,64]{4,3,2,1,0:T(8,128)} broadcast(f32[6,8,8]{2,1,0:T(8,128)S(1)} %bitcast.127), dimensions={0,1,3} | broadcast | bytes 6292992 | tf_op jit(solution)/shard_map/broadcast_in_dim | solution.py:34
  80.0 11.5 %reshape.1297 = f32[6,512,512]{2,1,0:T(8,128)} reshape(f32[6,8,64,8,64]{4,3,2,1,0:T(8,128)} %broadcast_in_dim.19) | data formatting | bytes 12582912 | tf_op jit(solution)/shard_map/reshape | solution.py:37
  91.5 2.5 copy.31
  94.1 2.6 copy.32
  101.7 2.6 copy.35
  104.3 2.6 copy.36
  106.8 2.6 copy.37
  117.0 2.6 copy.41
  119.6 2.5 copy.42
  125.3 12.8 %fusion.1 = bf16[3072,512]{1,0:T(8,128)(2,1)} fusion(f32[512,512]{1,0:T(8,128)S(1)} %copy.45, f32[3072]{0:T(1024)S(1)} %mul.935, f32[512,512]{1,0:T(8,128)S(1)} %copy.44, f32[3072]{0:T(1024)S(1)} %mul.929, f32[512,512]{1,0:T(8,128)} %copy.43, f32[3072]{0:T(1024)S(1)} %mul.923, f32[512,512]{1,0:T(8,128)} %copy.42, f32[3072]{0:T(1024)S(1)} %mul.917, ...), kind=kLoop, calls=%fused_computation.2 | loop fusion | flops 47185920 | bytes 19058688 | tf_op jit(solution)/shard_map/convert_element_type | solution.py:21
  138.5 10.5 %add_convert_fusion.1 = bf16[6,512,512]{2,1,0:T(8,128)(2,1)S(1)} fusion(f32[512,512]{1,0:T(8,128)} %copy.25, f32[6]{0:T(128)S(1)} %get-tuple-element.18, f32[512,512]{1,0:T(8,128)} %copy.24, f32[6]{0:T(128)S(1)} %get-tuple-element.19, f32[512,512]{1,0:T(8,128)} %copy.23, f32[6]{0:T(128)S(1)} %get-tuple-element.6, f32[512,512]{1,0:T(8,128)} %copy.22, ...), kind=kLoop, calls=%fused_computation.33 | loop fusion | flops 47185920 | bytes 18874728 | tf_op jit(solution)/shard_map/convert_element_type | solution.py:21
  149.1 3.9 %convolution_convert_fusion = bf16[512,3072]{1,0:T(8,128)(2,1)S(1)} fusion(bf16[512,3072]{0,1:T(8,128)(2,1)} %bitcast.125, bf16[512,2,512]{2,0,1:T(8,128)(2,1)} %all-gather.2.cloned.1.call-done, s32[]{:T(128)S(6)} %select_n.17), kind=kOutput, calls=%fused_computation.34 | convolution fusion | flops 1612185600 | bytes 6815748 | tf_op jit(solution)/shard_map/dot_general | solution.py:67
  155.5 4.7 %copy.27 = bf16[512,3072]{0,1:T(8,128)(2,1)} copy(bf16[512,3072]{1,0:T(8,128)(2,1)} %pad_dynamic-slice_fusion.1) | data formatting | bytes 6291456 | tf_op jit(solution)/shard_map/dynamic_slice | solution.py:30
  160.3 6.2 %multiply_reduce_fusion = f32[512,512]{1,0:T(8,128)S(1)} fusion(f32[6,512,512]{2,1,0:T(8,128)} %reshape.1297, bf16[6,512,512]{2,1,0:T(8,128)(2,1)S(1)} %add_convert_fusion.1, bf16[512,6,512]{0,2,1:T(8,128)(2,1)} %bitcast.124), kind=kOutput, calls=%fused_computation.31 | convolution fusion | flops 1613496320 | bytes 13631488 | tf_op jit(solution)/shard_map/kba,bkc->kac/dot_general | solution.py:33
  166.8 4.0 %fusion.18 = bf16[6,512,512]{2,1,0:T(8,128)(2,1)} fusion(bf16[6,512,512]{2,1,0:T(8,128)(2,1)S(1)} %add_convert_fusion.1, f32[6,512,512]{2,1,0:T(8,128)S(1)} %bitcast.123, f32[512,512]{1,0:T(8,128)S(1)} %fusion.20), kind=kOutput, calls=%fused_computation.40 | convolution fusion | flops 1615331328 | bytes 13631488 | tf_op jit(solution)/shard_map/kab,kbc->akc/dot_general | solution.py:41
  170.8 4.5 %fusion.15 = f32[512,512]{1,0:T(8,128)S(1)} fusion(bf16[3072,512]{1,0:T(8,128)(2,1)S(1)} %copy-done, s32[]{:T(128)S(6)} %select_n.19, bf16[512,3072]{0,1:T(8,128)(2,1)} %bitcast.126), kind=kOutput, calls=%fused_computation.37 | convolution fusion | flops 1610612736 | bytes 7340036 | tf_op jit(solution)/shard_map/dot_general | solution.py:48
  177.6 101.0 %all-reduce.4.cloned.1.call-done = f32[512,2,512]{2,1,0:T(2,128)} async-done(((f32[512,2,512]{2,1,0:T(2,128)}), f32[512,2,512]{2,1,0:T(2,128)}) %all-reduce.4.cloned.1.call-update) | async-done | bytes 2097168 | tf_op jit(solution)/shard_map/psum | solution.py:71
  (74 shorter events, 34.3 us)
Async XLA Ops:
  6.5 142.5 %all-gather.2.cloned.1.call-start = ((), (), s32[]{:S(2)}) async-start(), calls=%async_computation | async-start | bytes 1114112 | tf_op jit(solution)/shard_map/all_gather | solution.py:65
  8.1 270.5 %all-reduce.4.cloned.1.call-start = ((), (), s32[]{:S(2)}) async-start(), calls=%async_computation.1 | async-start | bytes 4194304 | tf_op jit(solution)/shard_map/psum | solution.py:71
  10.2 7.5 %copy-start.3 = (bf16[6,15]{1,0:T(8,128)(2,1)S(1)}, bf16[6,15]{1,0:T(8,128)(2,1)}, u32[]{:S(2)}) copy-start(bf16[6,15]{1,0:T(8,128)(2,1)} %param.15) | copy-start | bytes 544
  59.2 15.3 %copy-start.5 = (f32[1,6,8,8]{3,2,1,0:T(8,128)S(1)}, f32[1,6,8,8]{3,2,1,0:T(8,128)}, u32[]{:S(2)}) copy-start(f32[1,6,8,8]{3,2,1,0:T(8,128)} %param.11) | copy-start | bytes 4612
  125.3 12.9 %copy-start.4 = (bf16[6,15]{1,0:T(8,128)(2,1)S(1)}, bf16[6,15]{1,0:T(8,128)(2,1)}, u32[]{:S(2)}) copy-start(bf16[6,15]{1,0:T(8,128)(2,1)} %param.14) | copy-start | bytes 544
  160.3 6.5 %slice-start = ((s8[6291456]{0:T(1024)(128)(4,1)}), s8[4194304]{0:T(1024)(128)(4,1)S(1)}, s32[]{:S(2)}) async-start(s8[6291456]{0:T(1024)(128)(4,1)} %bitcast.122), calls=%async_computation.2 | async-start | bytes 8388608
  160.3 6.2 %copy-start.1 = (s32[1,512,512]{2,1,0:T(8,128)S(1)}, s32[1,512,512]{2,1,0:T(8,128)}, u32[]{:S(2)}) copy-start(s32[1,512,512]{2,1,0:T(8,128)} %param.10) | copy-start | bytes 3145732
  160.3 6.2 %copy-start.2 = (bf16[1,512,512]{2,1,0:T(8,128)(2,1)S(1)}, bf16[1,512,512]{2,1,0:T(8,128)(2,1)}, u32[]{:S(2)}) copy-start(bf16[1,512,512]{2,1,0:T(8,128)(2,1)} %param.9) | copy-start | bytes 1572868
  160.3 6.5 %slice-start.1 = ((s8[6291456]{0:T(1024)(128)(4,1)}), s8[2097152]{0:T(1024)(128)(4,1)S(1)}, s32[]{:S(2)}) async-start(s8[6291456]{0:T(1024)(128)(4,1)} %bitcast.122), calls=%async_computation.3 | async-start | bytes 4194304
  166.8 4.0 %copy-start = (bf16[3072,512]{1,0:T(8,128)(2,1)S(1)}, bf16[3072,512]{1,0:T(8,128)(2,1)}, u32[]{:S(2)}) copy-start(bf16[3072,512]{1,0:T(8,128)(2,1)} %fusion.1) | copy-start | bytes 9437188
Sparse Core Ops, SparseCore 0:
  9.5 40.5 all-gather.1
  177.7 100.8 all-reduce.3
where the time goes:
time: 289 us; the launch traced here: 287 us
  local copies, waits for them, and re-layouts  101 us (35%)
  waiting for transfers between devices  101 us (35%)
  other arithmetic  50.1 us (17%)
  matrix products  18.5 us (6%)
  between operations  16.4 us (6%)
    psum x1, waiting for transfers between devices, per_device(): lax.psum(back_rows(padded_back, back_stack, row_shift, patch_index, patch...  101 us
    convert_element_type x30, local copies, waits for them, and re-layouts, band_stack(): matches = ((offset == tap_index) & inside).astype(jnp.float32)  70.9 us
    convert_element_type x3, other arithmetic, band_stack(): return running.astype(jnp.bfloat16)  31.8 us
    convert_element_type x2, other arithmetic, band_stack(): matches = ((offset == tap_index) & inside).astype(jnp.float32)  14.4 us
    reshape x1, local copies, waits for them, and re-layouts, exposure_back(): mix_full = jnp.broadcast_to(blur_weights[:, :, None, :, None], (basis_cou...  11.5 us
    dynamic_slice x2, local copies, waits for them, and re-layouts, exposure_back(): lax.dynamic_slice_in_dim(padded, DMAX + row_shift, extent, 0)  7.27 us
    dot_general x1, matrix products, exposure_back(): jnp.einsum('kba,bkc->kac', column_band, shifted, preferred_element_type=j...  6.17 us
  transfers between devices with their start and end apart: 2, of which 1 were waited for; matrix products, arithmetic and copies ran while one was open for 48% of the time, Pallas kernels for 0%

commit v1 on v0

--- a/solution.py
+++ b/solution.py
@@ -68,8 +68,12 @@
     padded_back = exposure_back(
         rowed, observed[0], pixel_mask[0], blur_mix[0], row_shift, column_band
     )
-    complete = lax.psum(
-        back_rows(padded_back, back_stack, row_shift, patch_index, patch_count, 0, extent), "exp"
+    complete = jnp.sum(
+        lax.all_gather(
+            back_rows(padded_back, back_stack, row_shift, patch_index, patch_count, 0, extent),
+            "exp",
+        ),
+        axis=0,
     )
     return lax.dynamic_slice_in_dim(complete, lax.axis_index("exp") * band_rows, band_rows, 0)
 

time: 289 us -> 370 us (1.28)
  waiting for transfers between devices: 101 us -> 171 us
  other arithmetic: 50.1 us -> 62.2 us
    all_gather x0 -> x1, waiting for transfers between devices: none -> 171 us  [per_device(): lax.all_gather(back_rows(padded_back, back_stack, row_shift, patch_index,...]
    psum x1 -> x0, waiting for transfers between devices: 101 us -> none  [per_device(): lax.psum(back_rows(padded_back, back_stack, row_shift, patch_index, patch...]
    reduce_sum x0 -> x1, other arithmetic: none -> 12.7 us  [per_device(): jnp.sum(lax.all_gather(back_rows(padded_back, back_stack, row_shift, patc...]
  transfers between devices with their start and end apart: 2 -> 2, of which waited for: 1 -> 1; matrix products, arithmetic and copies ran while one was open for 48% -> 37% of each run, Pallas kernels for 0% -> 0%
where the time goes in v1:
time: 370 us; the launch traced here: 368 us
  waiting for transfers between devices  171 us (46%)
  local copies, waits for them, and re-layouts  100 us (27%)
  other arithmetic  62.2 us (17%)
  matrix products  18.5 us (5%)
  between operations  16.5 us (4%)
    all_gather x1, waiting for transfers between devices, per_device(): lax.all_gather(back_rows(padded_back, back_stack, row_shift, patch_index,...  171 us
    convert_element_type x30, local copies, waits for them, and re-layouts, band_stack(): matches = ((offset == tap_index) & inside).astype(jnp.float32)  70.9 us
    convert_element_type x3, other arithmetic, band_stack(): return running.astype(jnp.bfloat16)  31.8 us
    convert_element_type x2, other arithmetic, band_stack(): matches = ((offset == tap_index) & inside).astype(jnp.float32)  14.4 us
    reduce_sum x1, other arithmetic, per_device(): jnp.sum(lax.all_gather(back_rows(padded_back, back_stack, row_shift, patc...  12.7 us
    reshape x1, local copies, waits for them, and re-layouts, exposure_back(): mix_full = jnp.broadcast_to(blur_weights[:, :, None, :, None], (basis_cou...  11.5 us
  transfers between devices with their start and end apart: 2, of which 1 were waited for; matrix products, arithmetic and copies ran while one was open for 37% of the time, Pallas kernels for 0%

profile of v1, /device:TPU:0, one launch (start us, length us, event | category | flops | bytes accessed | tf_op | source)
XLA Modules:
  0.0 368.2 jit_solution(5421199459017871329)
XLA Ops:
  10.3 7.4 %fusion.68 = (f32[512,512]{0,1:T(8,128)S(1)}, f32[512,512]{0,1:T(8,128)}, f32[512,512]{0,1:T(8,128)S(1)}, f32[512,512]{0,1:T(8,128)S(1)}, f32[512,512]{0,1:T(8,1...) fusion(s32[]{:T(128)} %bitcast.3, ...), kind=kLoop, calls=%fused_computation.95 | loop fusion | flops 25165824 | bytes 31457796 | tf_op jit(solution)/shard_map/convert_element_type | solution.py:17
  18.0 8.4 %add_convert_fusion = bf16[512,6,512]{0,2,1:T(8,128)(2,1)} fusion(f32[512,512]{0,1:T(8,128)S(1)} %get-tuple-element.51, f32[6]{0:T(128)S(1)} %get-tuple-element.33, f32[512,512]{0,1:T(8,128)S(1)} %get-tuple-element.52, f32[6]{0:T(128)S(1)} %get-tuple-element.34, f32[512,512]{0,1:T(8,128)S(1)} %get-tuple-element.53, f32[6]{0:T(128)S(1)} %get-tuple-element.21, ...), kind=kLoop, calls=%fused_computation.32 | loop fusion | flops 47185920 | bytes 18874728 | tf_op jit(solution)/shard_map/convert_element_type | solution.py:21
  26.4 7.0 %fusion.128 = (f32[512,512]{0,1:T(8,128)}, f32[512,512]{0,1:T(8,128)}, f32[512,512]{0,1:T(8,128)}, f32[512,512]{0,1:T(8,128)}, f32[512,512]{0,1:T(8,128)}, /*ind...) fusion(pred[512]{0:T(512)(128)(4,1)S(1)} %iota_compare_fusion), kind=kLoop, calls=%fused_computation.155 | loop fusion | flops 12320768 | bytes 15729152 | tf_op jit(solution)/shard_map/convert_element_type | solution.py:17
  38.8 2.6 copy.82
  44.0 2.6 copy.84
  46.5 2.5 copy.85
  51.6 2.6 copy.87
  54.1 2.5 copy.88
  56.7 2.6 copy.89
  61.8 2.5 copy.91
  64.3 2.6 copy.92
  66.9 2.6 copy.93
  69.5 2.5 copy.94
  72.0 2.5 copy.95
  74.5 5.4 %broadcast_in_dim.19 = f32[6,8,64,8,64]{4,3,2,1,0:T(8,128)} broadcast(f32[6,8,8]{2,1,0:T(8,128)S(1)} %bitcast.127), dimensions={0,1,3} | broadcast | bytes 6292992 | tf_op jit(solution)/shard_map/broadcast_in_dim | solution.py:34
  80.0 11.5 %reshape.1300 = f32[6,512,512]{2,1,0:T(8,128)} reshape(f32[6,8,64,8,64]{4,3,2,1,0:T(8,128)} %broadcast_in_dim.19) | data formatting | bytes 12582912 | tf_op jit(solution)/shard_map/reshape | solution.py:37
  91.5 2.5 copy.101
  94.1 2.6 copy.102
  101.7 2.6 copy.105
  104.3 2.6 copy.106
  106.8 2.6 copy.107
  117.0 2.6 copy.111
  119.6 2.5 copy.112
  125.3 12.8 %fusion.1 = bf16[3072,512]{1,0:T(8,128)(2,1)} fusion(f32[512,512]{1,0:T(8,128)S(1)} %copy.115, f32[3072]{0:T(1024)S(1)} %mul.935, f32[512,512]{1,0:T(8,128)S(1)} %copy.114, f32[3072]{0:T(1024)S(1)} %mul.929, f32[512,512]{1,0:T(8,128)} %copy.113, f32[3072]{0:T(1024)S(1)} %mul.923, f32[512,512]{1,0:T(8,128)} %copy.112, f32[3072]{0:T(1024)S(1)} %mul.917, ...), kind=kLoop, calls=%fused_computation.2 | loop fusion | flops 47185920 | bytes 19058688 | tf_op jit(solution)/shard_map/convert_element_type | solution.py:21
  138.5 10.5 %add_convert_fusion.1 = bf16[6,512,512]{2,1,0:T(8,128)(2,1)S(1)} fusion(f32[512,512]{1,0:T(8,128)} %copy.95, f32[6]{0:T(128)S(1)} %get-tuple-element.18, f32[512,512]{1,0:T(8,128)} %copy.94, f32[6]{0:T(128)S(1)} %get-tuple-element.19, f32[512,512]{1,0:T(8,128)} %copy.93, f32[6]{0:T(128)S(1)} %get-tuple-element.6, f32[512,512]{1,0:T(8,128)} %copy.92, ...), kind=kLoop, calls=%fused_computation.33 | loop fusion | flops 47185920 | bytes 18874728 | tf_op jit(solution)/shard_map/convert_element_type | solution.py:21
  149.1 3.9 %convolution_convert_fusion = bf16[512,3072]{1,0:T(8,128)(2,1)S(1)} fusion(bf16[512,3072]{0,1:T(8,128)(2,1)} %bitcast.125, bf16[512,2,512]{2,0,1:T(8,128)(2,1)} %all-gather.3.cloned.1.call-done, s32[]{:T(128)S(6)} %select_n.24), kind=kOutput, calls=%fused_computation.34 | convolution fusion | flops 1612185600 | bytes 6815748 | tf_op jit(solution)/shard_map/dot_general | solution.py:67
  155.5 4.7 %copy.97 = bf16[512,3072]{0,1:T(8,128)(2,1)} copy(bf16[512,3072]{1,0:T(8,128)(2,1)} %pad_dynamic-slice_fusion.1) | data formatting | bytes 6291456 | tf_op jit(solution)/shard_map/dynamic_slice | solution.py:30
  160.3 6.2 %multiply_reduce_fusion = f32[512,512]{1,0:T(8,128)S(1)} fusion(f32[6,512,512]{2,1,0:T(8,128)} %reshape.1300, bf16[6,512,512]{2,1,0:T(8,128)(2,1)S(1)} %add_convert_fusion.1, bf16[512,6,512]{0,2,1:T(8,128)(2,1)} %bitcast.124), kind=kOutput, calls=%fused_computation.31 | convolution fusion | flops 1613496320 | bytes 13631488 | tf_op jit(solution)/shard_map/kba,bkc->kac/dot_general | solution.py:33
  166.8 4.0 %fusion.18 = bf16[6,512,512]{2,1,0:T(8,128)(2,1)} fusion(bf16[6,512,512]{2,1,0:T(8,128)(2,1)S(1)} %add_convert_fusion.1, f32[6,512,512]{2,1,0:T(8,128)S(1)} %bitcast.123, f32[512,512]{1,0:T(8,128)S(1)} %fusion.20), kind=kOutput, calls=%fused_computation.40 | convolution fusion | flops 1615331328 | bytes 13631488 | tf_op jit(solution)/shard_map/kab,kbc->akc/dot_general | solution.py:41
  170.8 4.5 %fusion.15 = f32[512,512]{1,0:T(8,128)S(1)} fusion(bf16[3072,512]{1,0:T(8,128)(2,1)S(1)} %copy-done, s32[]{:T(128)S(6)} %select_n.26, bf16[512,3072]{0,1:T(8,128)(2,1)} %bitcast.126), kind=kOutput, calls=%fused_computation.37 | convolution fusion | flops 1610612736 | bytes 7340036 | tf_op jit(solution)/shard_map/dot_general | solution.py:48
  177.0 170.9 %all-gather.5.cloned.1.call-done = f32[16,512,2,512]{3,1,2,0:T(8,128)} async-done(((f32[1,512,2,512]{3,1,2,0:T(8,128)}), f32[16,512,2,512]{3,1,2,0:T(8,128)}) %all-gather.5.cloned.1.call-update) | async-done | bytes 33554448 | tf_op jit(solution)/shard_map/all_gather | solution.py:72
  347.9 12.7 %reduce_sum.22 = f32[512,2,512]{2,0,1:T(8,128)S(1)} reduce(f32[16,512,2,512]{3,1,2,0:T(8,128)} %all-gather.5.cloned.1.call-done, f32[]{:T(128)} %constant.56.clone.1), dimensions={0}, to_apply=%region_1.2 | reduce | flops 7864320 | bytes 35651588 | tf_op jit(solution)/shard_map/reduce_sum | solution.py:71
  (76 shorter events, 35.5 us)
Async XLA Ops:
  6.5 142.5 %all-gather.3.cloned.1.call-start = ((), (), s32[]{:S(2)}) async-start(), calls=%async_computation | async-start | bytes 1114112 | tf_op jit(solution)/shard_map/all_gather | solution.py:65
  8.1 339.7 %all-gather.5.cloned.1.call-start = ((), (), s32[]{:S(2)}) async-start(), calls=%async_computation.1 | async-start | bytes 35651584 | tf_op jit(solution)/shard_map/all_gather | solution.py:72
  10.2 7.5 %copy-start.3 = (bf16[6,15]{1,0:T(8,128)(2,1)S(1)}, bf16[6,15]{1,0:T(8,128)(2,1)}, u32[]{:S(2)}) copy-start(bf16[6,15]{1,0:T(8,128)(2,1)} %param.15) | copy-start | bytes 544
  59.2 15.3 %copy-start.5 = (f32[1,6,8,8]{3,2,1,0:T(8,128)S(1)}, f32[1,6,8,8]{3,2,1,0:T(8,128)}, u32[]{:S(2)}) copy-start(f32[1,6,8,8]{3,2,1,0:T(8,128)} %param.11) | copy-start | bytes 4612
  125.3 12.9 %copy-start.4 = (bf16[6,15]{1,0:T(8,128)(2,1)S(1)}, bf16[6,15]{1,0:T(8,128)(2,1)}, u32[]{:S(2)}) copy-start(bf16[6,15]{1,0:T(8,128)(2,1)} %param.14) | copy-start | bytes 544
  160.3 6.5 %slice-start = ((s8[6291456]{0:T(1024)(128)(4,1)}), s8[4194304]{0:T(1024)(128)(4,1)S(1)}, s32[]{:S(2)}) async-start(s8[6291456]{0:T(1024)(128)(4,1)} %bitcast.122), calls=%async_computation.2 | async-start | bytes 8388608
  160.3 6.2 %copy-start.1 = (s32[1,512,512]{2,1,0:T(8,128)S(1)}, s32[1,512,512]{2,1,0:T(8,128)}, u32[]{:S(2)}) copy-start(s32[1,512,512]{2,1,0:T(8,128)} %param.10) | copy-start | bytes 3145732
  160.3 6.2 %copy-start.2 = (bf16[1,512,512]{2,1,0:T(8,128)(2,1)S(1)}, bf16[1,512,512]{2,1,0:T(8,128)(2,1)}, u32[]{:S(2)}) copy-start(bf16[1,512,512]{2,1,0:T(8,128)(2,1)} %param.9) | copy-start | bytes 1572868
  160.3 6.5 %slice-start.1 = ((s8[6291456]{0:T(1024)(128)(4,1)}), s8[2097152]{0:T(1024)(128)(4,1)S(1)}, s32[]{:S(2)}) async-start(s8[6291456]{0:T(1024)(128)(4,1)} %bitcast.122), calls=%async_computation.3 | async-start | bytes 4194304
  166.8 4.0 %copy-start = (bf16[3072,512]{1,0:T(8,128)(2,1)S(1)}, bf16[3072,512]{1,0:T(8,128)(2,1)}, u32[]{:S(2)}) copy-start(bf16[3072,512]{1,0:T(8,128)(2,1)} %fusion.1) | copy-start | bytes 9437188
Sparse Core Ops, SparseCore 0:
  9.5 40.5 all-gather.2
  177.1 170.7 all-gather.4
